TPU v7x, 512 devices: a whole 4x4x16 slice. The times are simulated.
512 devices in a mesh: dp: 32 (over z, core), tensor: 16 (over y, x).
Axes of the slice: x: 4, y: 4, z: 16, core: 2. Of those that a mesh axis runs over, the one named last changes fastest.
Arguments:
- dout: bfloat16 [12288, 5120], P(('dp', 'tensor')), may hold values from -0.75 to 0.75
- attn_ctx: bfloat16 [12288, 5120], P('dp', 'tensor'), may hold values from -6 to 6
- mlp_hidden: bfloat16 [12288, 13824], P('dp', 'tensor'), may hold values from -6 to 6
- w_out: bfloat16 [5120, 5120], P('tensor', 'dp'), may hold values from -0.078125 to 0.078125
- w_down: bfloat16 [13824, 5120], P('tensor', 'dp'), may hold values from -0.0546875 to 0.0546875
- head_logits: float32 [40], replicated, may hold values from -2 to 3
- unit_logits: float32 [13824], P('tensor'), may hold values from -2 to 3
- head_noise: float32 [40], replicated, may hold values from 0.001 to 0.999
- unit_noise: float32 [13824], P('tensor'), may hold values from 0.001 to 0.999
- linear_mult: float32 [1], replicated, may hold values from 100 to 300
- square_mult: float32 [1], replicated, may hold values from 1 to 4
- target: float32 [1], replicated, may hold values from 40 to 70
Outputs:
- ctx_grad: bfloat16 [12288, 5120], P('dp', 'tensor')
- hidden_grad: bfloat16 [12288, 13824], P('dp', 'tensor')
- head_grad: float32 [40], replicated
- unit_grad: float32 [13824], P('tensor')
All inputs are finite; a program needn't handle non-finite values.
Results may differ from a plain program's by a relative error of at most 0.001.
Values may be sent and summed in bfloat16 or wider, within the bound.
No kernel may reach another device: no remote copies, remote signals or barrier semaphores. Data moves between devices by JAX's collectives and lax.ppermute only.
A program may use at most 64 MiB of HBM per device.

v0:
```python
import jax
import jax.numpy as jnp
from jax import lax
from jax.sharding import PartitionSpec as P

H = 40
HEAD = 128
FF = 13824
low_end = -0.1
high_end = 1.1
temper = 2.0 / 3.0


def concrete(logits, noise):
    shape_s = jax.nn.sigmoid((jnp.log(noise) - jnp.log(1.0 - noise) + logits) / temper)
    stretched = shape_s * (high_end - low_end) + low_end
    gate = jnp.clip(stretched, 0.0, 1.0)
    inside = jnp.logical_and(stretched > 0.0, stretched < 1.0)
    slope = jnp.where(
        inside, (high_end - low_end) / temper * shape_s * (1.0 - shape_s), 0.0 * shape_s
    )
    return (gate, slope)


def open_prob(logits):
    return jax.nn.sigmoid(logits - temper * jnp.log(-low_end / high_end))


def local(
    dout,
    attn_ctx,
    mlp_hidden,
    w_out,
    w_down,
    head_logits,
    unit_logits,
    head_noise,
    unit_noise,
    linear_mult,
    square_mult,
    target,
):
    head_gate, head_slope = concrete(head_logits, head_noise)
    unit_gate, unit_slope = concrete(unit_logits, unit_noise)
    col_count = attn_ctx.shape[1]
    head_total = head_logits.shape[0]
    tensor_index = lax.axis_index("tensor")
    columns = tensor_index * col_count + lax.iota(jnp.int32, col_count)
    owner = columns // HEAD
    member = (owner[:, None] == lax.iota(jnp.int32, head_total)[None, :]).astype(jnp.float32)
    col_gate = jnp.dot(member, head_gate, precision=lax.Precision.HIGHEST)
    full_rows = lax.all_gather(dout, "tensor", axis=0, tiled=True)
    dims = (((1,), (1,)), ((), ()))

    def contract(piece):
        return lax.dot_general(full_rows, piece, dims, preferred_element_type=jnp.float32)

    ctx_pre = contract(lax.all_gather(w_out, "dp", axis=1, tiled=True))
    hid_pre = contract(lax.all_gather(w_down, "dp", axis=1, tiled=True))
    ctx_grad = (ctx_pre * col_gate[None, :]).astype(jnp.bfloat16)
    hidden_grad = (hid_pre * unit_gate[None, :]).astype(jnp.bfloat16)
    col_part = jnp.sum(attn_ctx.astype(jnp.float32) * ctx_pre, axis=0)
    unit_part = jnp.sum(mlp_hidden.astype(jnp.float32) * hid_pre, axis=0)
    head_part = jnp.dot(col_part, member, precision=lax.Precision.HIGHEST)
    p_head = open_prob(head_logits)
    p_unit = open_prob(unit_logits)
    local_mass = jnp.sum(p_unit)
    unit_data = lax.psum(unit_part, "dp")
    head_data = lax.psum(head_part, ("dp", "tensor"))
    unit_mass = lax.psum(local_mass, "tensor")
    denom = 4.0 * HEAD * H + 3.0 * FF
    size = 100.0 * (4.0 * HEAD * jnp.sum(p_head) + 3.0 * unit_mass) / denom
    factor = linear_mult[0] + 2.0 * square_mult[0] * (size - target[0])
    head_grad = head_data * head_slope + factor * (400.0 * HEAD / denom) * p_head * (1.0 - p_head)
    unit_grad = unit_data * unit_slope + factor * (300.0 / denom) * p_unit * (1.0 - p_unit)
    return (ctx_grad, hidden_grad, head_grad, unit_grad)


def solution(mesh):
    placed = (
        P(("dp", "tensor"), None),
        P("dp", "tensor"),
        P("dp", "tensor"),
        P("tensor", "dp"),
        P("tensor", "dp"),
        P(),
        P("tensor"),
        P(),
        P("tensor"),
        P(),
        P(),
        P(),
    )
    return jax.shard_map(
        local,
        mesh=mesh,
        in_specs=placed,
        out_specs=(P("dp", "tensor"), P("dp", "tensor"), P(), P("tensor")),
        check_vma=False,
    )
```

profile of v0, /device:TPU:1, one launch (start us, length us, event | category | flops | bytes accessed | tf_op | source)
XLA Modules:
  0.0 329.6 jit_solution(5489138382124432926)
XLA Ops:
  7.2 0.0 all-gather.6.cloned.1.call-start
  7.2 0.7 all-gather.6.cloned.1.call-update
  7.9 0.0 all-gather.4.cloned.1.call-start
  7.9 0.7 all-gather.4.cloned.1.call-update
  8.6 0.0 all-gather.8.cloned.1.call-start
  8.7 0.7 all-gather.8.cloned.1.call-update
  9.4 1.3 fusion.2
  10.7 34.9 %psum.22 = f32[]{:T(128)} all-reduce(f32[]{:T(128)} %get-tuple-element.11), channel_id=1, replica_groups=mesh['dp'=32,'tensor'=16] {'tensor'}, use_global_device_ids=true, to_apply=%region_4.5 | all-reduce | flops 1 | bytes 8 | tf_op jit(solution)/shard_map/psum | solution.py:70
  48.2 1.3 fusion.17
  50.1 0.0 copy-start.2
  50.1 0.0 copy-start.3
  50.2 0.0 copy-start.4
  50.2 38.7 %all-gather.6.cloned.1.call-done = bf16[320,5120]{0,1:T(8,128)(2,1)} async-done(((bf16[320,160]{0,1:T(8,128)(2,1)}), bf16[320,5120]{0,1:T(8,128)(2,1)}) %all-gather.6.cloned.1.call-update) | async-done | bytes 3276816 | tf_op jit(solution)/shard_map/all_gather | solution.py:58
  88.8 65.0 %all-gather.4.cloned.1.call-done = bf16[384,5120]{1,0:T(8,128)(2,1)} async-done(((bf16[24,5120]{1,0:T(8,128)(2,1)}), bf16[384,5120]{1,0:T(8,128)(2,1)}) %all-gather.4.cloned.1.call-update) | async-done | bytes 3932176 | tf_op jit(solution)/shard_map/all_gather | solution.py:52
  153.9 5.3 %multiply_reduce_fusion.1 = (f32[320]{0:T(512)S(1)}, f32[384,320]{0,1:T(8,128)S(1)}) fusion(bf16[384,320]{0,1:T(8,128)(2,1)} %param.13, bf16[384,5120]{1,0:T(8,128)(2,1)} %all-gather.4.cloned.1.call-done, bf16[320,5120]{0,1:T(8,128)(2,1)} %all-gather.6.cloned.1.call-done), kind=kOutput, calls=%fused_computation.4 | convolution fusion | flops 1258659584 | bytes 7947520 | tf_op jit(solution)/shard_map/dot_general | solution.py:56
  159.2 0.2 convolution_bitcast_fusion
  159.5 105.0 %psum.21 = f32[40]{0:T(128)S(1)} all-reduce(f32[40]{0:T(128)S(1)} %convolution_bitcast_fusion), channel_id=1, replica_groups=mesh['dp'=32,'tensor'=16] {'dp','tensor'}, use_global_device_ids=true, to_apply=%region_1.2 | all-reduce | flops 40 | bytes 320 | tf_op jit(solution)/shard_map/psum | solution.py:69
  264.5 0.0 copy-done.2
  264.5 0.0 copy-done.3
  264.5 0.5 multiply_add_fusion.2
  265.0 0.3 convolution_reduce_fusion
  265.3 0.8 multiply_convert_fusion.1
  266.1 0.0 all-gather.8.cloned.1.call-done
  266.2 0.0 copy-done.4
  266.2 0.0 copy-start
  266.2 0.0 copy-start.1
  266.2 10.5 %multiply_reduce_fusion = (f32[864]{0:T(1024)S(1)}, bf16[384,864]{0,1:T(8,128)(2,1)}) fusion(bf16[384,864]{0,1:T(8,128)(2,1)S(1)} %copy-done.4, f32[864]{0:T(1024)S(1)} %get-tuple-element.10, bf16[384,5120]{1,0:T(8,128)(2,1)} %all-gather.4.cloned.1.call-done, bf16[864,5120]{0,1:T(8,128)(2,1)} %all-gather.8.cloned.1.call-done), kind=kOutput, calls=%fused_computation | convolution fusion | flops 3399044352 | bytes 14113536 | tf_op jit(solution)/shard_map/dot_general | solution.py:56
  276.7 45.8 %psum.23 = f32[864]{0:T(1024)S(1)} all-reduce(f32[864]{0:T(1024)S(1)} %get-tuple-element.8), channel_id=1, replica_groups=mesh['dp'=32,'tensor'=16] {'dp'}, use_global_device_ids=true, to_apply=%region_6.7 | all-reduce | flops 864 | bytes 6912 | tf_op jit(solution)/shard_map/psum | solution.py:68
  322.5 0.0 copy-done
  322.5 0.0 copy-done.1
  322.5 0.6 multiply_add_fusion
  (2 shorter events, 0.0 us)
Async XLA Ops:
  7.2 81.7 %all-gather.6.cloned.1.call-start = ((), (), s32[]{:S(2)}) async-start(), calls=%async_computation.1 | async-start | bytes 4055040 | tf_op jit(solution)/shard_map/all_gather | solution.py:58
  7.9 146.0 %all-gather.4.cloned.1.call-start = ((), (), s32[]{:S(2)}) async-start(), calls=%async_computation | async-start | bytes 4177920 | tf_op jit(solution)/shard_map/all_gather | solution.py:52
  8.6 257.5 %all-gather.8.cloned.1.call-start = ((), (), s32[]{:S(2)}) async-start(), calls=%async_computation.2 | async-start | bytes 9461760 | tf_op jit(solution)/shard_map/all_gather | solution.py:59
  50.1 214.4 %copy-start.2 = (f32[40]{0:T(128)S(1)}, f32[40]{0:T(128)}, u32[]{:S(2)}) copy-start(f32[40]{0:T(128)} %param.17) | copy-start | bytes 484
  50.1 214.4 %copy-start.3 = (f32[40]{0:T(128)S(1)}, f32[40]{0:T(128)}, u32[]{:S(2)}) copy-start(f32[40]{0:T(128)} %param.19) | copy-start | bytes 484
  50.2 216.0 %copy-start.4 = (bf16[384,864]{0,1:T(8,128)(2,1)S(1)}, bf16[384,864]{0,1:T(8,128)(2,1)}, u32[]{:S(2)}) copy-start(bf16[384,864]{0,1:T(8,128)(2,1)} %param.14) | copy-start | bytes 1990660
  266.2 56.3 %copy-start = (f32[864]{0:T(1024)S(1)}, f32[864]{0:T(1024)}, u32[]{:S(2)}) copy-start(f32[864]{0:T(1024)} %param.18) | copy-start | bytes 10372
  266.2 56.3 %copy-start.1 = (f32[864]{0:T(1024)S(1)}, f32[864]{0:T(1024)}, u32[]{:S(2)}) copy-start(f32[864]{0:T(1024)} %param.20) | copy-start | bytes 10372
Sparse Core Ops, SparseCore 0:
  10.1 78.6 all-gather.5
  91.8 61.9 all-gather.3
  156.0 80.5 all-gather.7
where the time goes:
time: 330 us
  blocking collectives  186 us (56%)
  waiting for transfers between devices  106 us (32%)
  between operations  17.1 us (5%)
  matrix products  16.4 us (5%)
  other arithmetic  4.6 us (1%)
    psum x1, blocking collectives, local(): head_data = lax.psum(head_part, ('dp', 'tensor'))  105 us
    all_gather x1, waiting for transfers between devices, local(): full_rows = lax.all_gather(dout, 'tensor', axis=0, tiled=True)  65 us
    psum x1, blocking collectives, local(): unit_data = lax.psum(unit_part, 'dp')  45.8 us
    all_gather x1, waiting for transfers between devices, local(): ctx_pre = contract(lax.all_gather(w_out, 'dp', axis=1, tiled=True))  38.7 us
    psum x1, blocking collectives, local(): unit_mass = lax.psum(local_mass, 'tensor')  34.9 us
    dot_general x2, matrix products, contract(): lax.dot_general(full_rows, piece, dims, preferred_element_type=jnp.float32)  15.9 us
  transfers between devices with their start and end apart: 3, of which 2 were waited for; matrix products, arithmetic and copies ran while one was open for 3% of the time, Pallas kernels for 0%

commit v1 on v0

--- a/solution.py
+++ b/solution.py
@@ -40,6 +40,14 @@
     square_mult,
     target,
 ):
+
+    def panels_state(incoming_x, axis_id="dp"):
+        inter = incoming_x
+        axis_n = lax.axis_size(axis_id)
+        for ix in [[(q, q ^ u) for q in range(axis_n)] for u in (1, 2, 4, 8, 16) if u < axis_n]:
+            inter = inter + lax.ppermute(inter, axis_id, ix)
+        return inter
+
     head_gate, head_slope = concrete(head_logits, head_noise)
     unit_gate, unit_slope = concrete(unit_logits, unit_noise)
     col_count = attn_ctx.shape[1]
@@ -65,7 +73,7 @@
     p_head = open_prob(head_logits)
     p_unit = open_prob(unit_logits)
     local_mass = jnp.sum(p_unit)
-    unit_data = lax.psum(unit_part, "dp")
+    unit_data = panels_state(unit_part)
     head_data = lax.psum(head_part, ("dp", "tensor"))
     unit_mass = lax.psum(local_mass, "tensor")
     denom = 4.0 * HEAD * H + 3.0 * FF

time: 330 us -> 382 us (1.16)
  waiting for transfers between devices: 106 us -> 185 us
  blocking collectives: 186 us -> 137 us
  starting transfers between devices: 0.11 us -> 19.2 us
    all_gather x1, waiting for transfers between devices: 0.01 us -> 81.7 us  [local(): hid_pre = contract(lax.all_gather(w_down, 'dp', axis=1, tiled=True))]
    psum x1 -> x0, blocking collectives: 45.8 us -> none  [local(): unit_data = lax.psum(unit_part, 'dp')]
    all_gather x1, waiting for transfers between devices: 65 us -> 31.4 us  [local(): full_rows = lax.all_gather(dout, 'tensor', axis=0, tiled=True)]
    all_gather x1, waiting for transfers between devices: 38.7 us -> 58.2 us  [local(): ctx_pre = contract(lax.all_gather(w_out, 'dp', axis=1, tiled=True))]
    ppermute x0 -> x5, starting transfers between devices: none -> 19.1 us  [panels_state(): inter = inter + lax.ppermute(inter, axis_id, ix)]
    ppermute x0 -> x5, waiting for transfers between devices: none -> 11.5 us  [panels_state(): inter = inter + lax.ppermute(inter, axis_id, ix)]
  transfers between devices with their start and end apart: 3 -> 8, of which waited for: 2 -> 6; matrix products, arithmetic and copies ran while one was open for 3% -> 5% of each run, Pallas kernels for 0% -> 0%
where the time goes in v1:
time: 382 us; the launch traced here: 379 us
  waiting for transfers between devices  185 us (48%)
  blocking collectives  137 us (36%)
  starting transfers between devices  19.2 us (5%)
  between operations  17.1 us (4%)
  matrix products  16.4 us (4%)
  other arithmetic  4.61 us (1%)
    psum x1, blocking collectives, local(): head_data = lax.psum(head_part, ('dp', 'tensor'))  102 us
    all_gather x1, waiting for transfers between devices, local(): hid_pre = contract(lax.all_gather(w_down, 'dp', axis=1, tiled=True))  81.7 us
    all_gather x1, waiting for transfers between devices, local(): ctx_pre = contract(lax.all_gather(w_out, 'dp', axis=1, tiled=True))  58.2 us
    psum x1, blocking collectives, local(): unit_mass = lax.psum(local_mass, 'tensor')  35 us
    all_gather x1, waiting for transfers between devices, local(): full_rows = lax.all_gather(dout, 'tensor', axis=0, tiled=True)  31.4 us
    ppermute x5, starting transfers between devices, panels_state(): inter = inter + lax.ppermute(inter, axis_id, ix)  19.1 us
    dot_general x2, matrix products, contract(): lax.dot_general(full_rows, piece, dims, preferred_element_type=jnp.float32)  15.9 us
    ppermute x5, waiting for transfers between devices, panels_state(): inter = inter + lax.ppermute(inter, axis_id, ix)  11.5 us
  transfers between devices with their start and end apart: 8, of which 6 were waited for; matrix products, arithmetic and copies ran while one was open for 5% of the time, Pallas kernels for 0%

profile of v1, /device:TPU:1, one launch (start us, length us, event | category | flops | bytes accessed | tf_op | source)
XLA Modules:
  0.0 378.9 jit_solution(4247431754333246797)
XLA Ops:
  7.2 0.0 all-gather.4.cloned.1.call-start
  7.2 0.7 all-gather.4.cloned.1.call-update
  7.9 0.0 all-gather.8.cloned.1.call-start
  7.9 0.7 all-gather.8.cloned.1.call-update
  8.6 0.0 all-gather.6.cloned.1.call-start
  8.7 0.7 all-gather.6.cloned.1.call-update
  9.4 1.3 fusion.2
  10.7 35.0 %psum.15 = f32[]{:T(128)} all-reduce(f32[]{:T(128)} %get-tuple-element.11), channel_id=1, replica_groups=mesh['dp'=32,'tensor'=16] {'tensor'}, use_global_device_ids=true, to_apply=%region_4.5 | all-reduce | flops 1 | bytes 8 | tf_op jit(solution)/shard_map/psum | solution.py:78
  48.3 1.3 fusion.17
  50.2 31.4 %all-gather.4.cloned.1.call-done = bf16[384,5120]{1,0:T(8,128)(2,1)} async-done(((bf16[24,5120]{1,0:T(8,128)(2,1)}), bf16[384,5120]{1,0:T(8,128)(2,1)}) %all-gather.4.cloned.1.call-update) | async-done | bytes 3932176 | tf_op jit(solution)/shard_map/all_gather | solution.py:60
  81.6 81.7 %all-gather.8.cloned.1.call-done = bf16[864,5120]{0,1:T(8,128)(2,1)} async-done(((bf16[864,160]{0,1:T(8,128)(2,1)}), bf16[864,5120]{0,1:T(8,128)(2,1)}) %all-gather.8.cloned.1.call-update) | async-done | bytes 8847376 | tf_op jit(solution)/shard_map/all_gather | solution.py:67
  163.3 10.5 %multiply_reduce_fusion = (f32[864]{0:T(1024)S(1)}, bf16[384,864]{0,1:T(8,128)(2,1)}) fusion(bf16[384,864]{0,1:T(8,128)(2,1)} %param.14, f32[864]{0:T(1024)S(1)} %get-tuple-element.10, bf16[384,5120]{1,0:T(8,128)(2,1)} %all-gather.4.cloned.1.call-done, bf16[864,5120]{0,1:T(8,128)(2,1)} %all-gather.8.cloned.1.call-done), kind=kOutput, calls=%fused_computation | convolution fusion | flops 3399044352 | bytes 14113536 | tf_op jit(solution)/shard_map/dot_general | solution.py:64
  173.8 2.3 collective-permute-start
  176.2 58.2 %all-gather.6.cloned.1.call-done = bf16[320,5120]{0,1:T(8,128)(2,1)} async-done(((bf16[320,160]{0,1:T(8,128)(2,1)}), bf16[320,5120]{0,1:T(8,128)(2,1)}) %all-gather.6.cloned.1.call-update) | async-done | bytes 3276816 | tf_op jit(solution)/shard_map/all_gather | solution.py:66
  234.4 5.3 %multiply_reduce_fusion.1 = (f32[320]{0:T(512)S(1)}, f32[384,320]{0,1:T(8,128)S(1)}) fusion(bf16[384,320]{0,1:T(8,128)(2,1)S(1)} %copy-done.4, bf16[384,5120]{1,0:T(8,128)(2,1)} %all-gather.4.cloned.1.call-done, bf16[320,5120]{0,1:T(8,128)(2,1)} %all-gather.6.cloned.1.call-done), kind=kOutput, calls=%fused_computation.4 | convolution fusion | flops 1258659584 | bytes 7947520 | tf_op jit(solution)/shard_map/dot_general | solution.py:64
  239.7 0.0 collective-permute-done
  239.7 3.4 collective-permute-start.1
  243.1 0.2 convolution_bitcast_fusion
  243.4 101.9 %psum.14 = f32[40]{0:T(128)S(1)} all-reduce(f32[40]{0:T(128)S(1)} %convolution_bitcast_fusion), channel_id=1, replica_groups=mesh['dp'=32,'tensor'=16] {'dp','tensor'}, use_global_device_ids=true, to_apply=%region_1.2 | all-reduce | flops 40 | bytes 320 | tf_op jit(solution)/shard_map/psum | solution.py:77
  345.2 0.0 collective-permute-done.1
  345.2 1.9 collective-permute-start.2
  347.2 0.0 copy-done.2
  347.2 0.0 copy-done.3
  347.2 0.5 multiply_add_fusion.2
  347.7 2.8 collective-permute-done.2
  350.5 4.2 %collective-permute-start.3 = (f32[864]{0:T(1024)S(1)}, f32[864]{0:T(1024)S(1)}, u32[]{:S(2)}, u32[]{:S(2)}) collective-permute-start(f32[864]{0:T(1024)S(1)} %add.95), channel_id=1, source_target_pairs={{0,128},{16,144},{32,160},{48,176},{64,192},{80,208},{96,224},{112... | collective-permute-start | bytes 10376 | tf_op jit(solution)/shard_map/ppermute | solution.py:48
  354.7 0.3 convolution_reduce_fusion
  355.0 3.8 collective-permute-done.3
  358.7 7.3 %collective-permute-start.4 = (f32[864]{0:T(1024)S(1)}, f32[864]{0:T(1024)S(1)}, u32[]{:S(2)}, u32[]{:S(2)}) collective-permute-start(f32[864]{0:T(1024)S(1)} %add.96), channel_id=1, source_target_pairs={{0,256},{16,272},{32,288},{48,304},{64,320},{80,336},{96,352},{112... | collective-permute-start | bytes 10376 | tf_op jit(solution)/shard_map/ppermute | solution.py:48
  366.0 0.8 multiply_convert_fusion.1
  366.8 5.0 %collective-permute-done.4 = f32[864]{0:T(1024)S(1)} collective-permute-done((f32[864]{0:T(1024)S(1)}, f32[864]{0:T(1024)S(1)}, u32[]{:S(2)}, u32[]{:S(2)}) %collective-permute-start.4) | collective-permute-done | bytes 3488 | tf_op jit(solution)/shard_map/ppermute | solution.py:48
  371.8 0.6 multiply_add_fusion
  (14 shorter events, 0.0 us)
Async XLA Ops:
  7.2 74.4 %all-gather.4.cloned.1.call-start = ((), (), s32[]{:S(2)}) async-start(), calls=%async_computation | async-start | bytes 4177920 | tf_op jit(solution)/shard_map/all_gather | solution.py:60
  7.9 155.4 %all-gather.8.cloned.1.call-start = ((), (), s32[]{:S(2)}) async-start(), calls=%async_computation.2 | async-start | bytes 9461760 | tf_op jit(solution)/shard_map/all_gather | solution.py:67
  8.6 225.7 %all-gather.6.cloned.1.call-start = ((), (), s32[]{:S(2)}) async-start(), calls=%async_computation.1 | async-start | bytes 4055040 | tf_op jit(solution)/shard_map/all_gather | solution.py:66
  163.3 71.1 %copy-start.4 = (bf16[384,320]{0,1:T(8,128)(2,1)S(1)}, bf16[384,320]{0,1:T(8,128)(2,1)}, u32[]{:S(2)}) copy-start(bf16[384,320]{0,1:T(8,128)(2,1)} %param.13) | copy-start | bytes 737284
  173.8 173.3 %copy-start.2 = (f32[40]{0:T(128)S(1)}, f32[40]{0:T(128)}, u32[]{:S(2)}) copy-start(f32[40]{0:T(128)} %param.17) | copy-start | bytes 484
  173.8 173.3 %copy-start.3 = (f32[40]{0:T(128)S(1)}, f32[40]{0:T(128)}, u32[]{:S(2)}) copy-start(f32[40]{0:T(128)} %param.19) | copy-start | bytes 484
  173.8 198.0 %copy-start = (f32[864]{0:T(1024)S(1)}, f32[864]{0:T(1024)}, u32[]{:S(2)}) copy-start(f32[864]{0:T(1024)} %param.18) | copy-start | bytes 10372
  173.8 198.0 %copy-start.1 = (f32[864]{0:T(1024)S(1)}, f32[864]{0:T(1024)}, u32[]{:S(2)}) copy-start(f32[864]{0:T(1024)} %param.20) | copy-start | bytes 10372
  173.8 65.9 %collective-permute-start = (f32[864]{0:T(1024)S(1)}, f32[864]{0:T(1024)S(1)}, u32[]{:S(2)}, u32[]{:S(2)}) collective-permute-start(f32[864]{0:T(1024)S(1)} %get-tuple-element.8), channel_id=1, source_target_pairs={{0,16},{16,0},{32,48},{48,32},{64,80},{80,64},{96,112},{112,96},{1... | collective-permute-start | bytes 10376 | tf_op jit(solution)/shard_map/ppermute | solution.py:48
  239.7 105.5 %collective-permute-start.1 = (f32[864]{0:T(1024)S(1)}, f32[864]{0:T(1024)S(1)}, u32[]{:S(2)}, u32[]{:S(2)}) collective-permute-start(f32[864]{0:T(1024)S(1)} %add.93), channel_id=1, source_target_pairs={{0,32},{16,48},{32,0},{48,16},{64,96},{80,112},{96,64},{112,80},{1... | collective-permute-start | bytes 10376 | tf_op jit(solution)/shard_map/ppermute | solution.py:48
  345.2 5.2 %collective-permute-start.2 = (f32[864]{0:T(1024)S(1)}, f32[864]{0:T(1024)S(1)}, u32[]{:S(2)}, u32[]{:S(2)}) collective-permute-start(f32[864]{0:T(1024)S(1)} %add.94), channel_id=1, source_target_pairs={{0,64},{16,80},{32,96},{48,112},{64,0},{80,16},{96,32},{112,48},{1... | collective-permute-start | bytes 10376 | tf_op jit(solution)/shard_map/ppermute | solution.py:48
  350.5 8.2 %collective-permute-start.3 = (f32[864]{0:T(1024)S(1)}, f32[864]{0:T(1024)S(1)}, u32[]{:S(2)}, u32[]{:S(2)}) collective-permute-start(f32[864]{0:T(1024)S(1)} %add.95), channel_id=1, source_target_pairs={{0,128},{16,144},{32,160},{48,176},{64,192},{80,208},{96,224},{112... | collective-permute-start | bytes 10376 | tf_op jit(solution)/shard_map/ppermute | solution.py:48
  358.7 13.1 %collective-permute-start.4 = (f32[864]{0:T(1024)S(1)}, f32[864]{0:T(1024)S(1)}, u32[]{:S(2)}, u32[]{:S(2)}) collective-permute-start(f32[864]{0:T(1024)S(1)} %add.96), channel_id=1, source_target_pairs={{0,256},{16,272},{32,288},{48,304},{64,320},{80,336},{96,352},{112... | collective-permute-start | bytes 10376 | tf_op jit(solution)/shard_map/ppermute | solution.py:48
Sparse Core Ops, SparseCore 0:
  11.0 70.5 all-gather.3
  83.7 79.5 all-gather.7
  165.4 68.8 all-gather.5
